TPU v7x, 128 devices: a whole 4x4x4 slice. The times are simulated.
128 devices in a mesh: cand: 16 (over z_lo, y, core), rel: 8 (over z_hi, x).
Axes of the slice: x: 4, y: 4, z: 4 (z_hi: 2, z_lo: 2; z = z_hi * 2 + z_lo), core: 2. Of those that a mesh axis runs over, the one named last changes fastest.
Arguments:
- source_rows: bfloat16 [262144, 512], P(('cand', 'rel')), may hold values from -24 to 24
- rel_ids: int32 [262144, 1], P(('cand', 'rel')), may hold values from 0 to 15; in each aligned block of 2048 rows (0 to 2047, 2048 to 4095, ...) at most 256 rows name the same one
- relations: bfloat16 [16, 512, 512], P('rel'), may hold values from -0.25 to 0.25
- entities: float32 [32768, 512], P(('cand', 'rel')), may hold values from -0.3 to 0.3
- pos_slot: int32 [262144], P(('cand', 'rel')), may hold values from 0 to 2047
- negatives: int32 [8, 262144, 16], P(None, ('cand', 'rel')), may hold values from 0 to 255
Outputs:
- updated_entities: float32 [32768, 512], P(('cand', 'rel'))
- source_grad: bfloat16 [262144, 512], P(('cand', 'rel'))
- relation_grad: float32 [512, 16, 512], P('cand', 'rel')
Inputs may be any that keep to these rules, and one draw needn't show every extreme that they name: `rel_ids`: in each aligned block of 2048 rows (the rows of one device) no relation is named by more than 256 rows, a bound that some block reaches.
All inputs are finite; a program needn't handle non-finite values.
Results may differ from a plain program's by a relative error of at most 0.019.
Values may be sent and summed in bfloat16 or wider, within the bound.
A program may use at most 128 MiB of HBM per device.

v0:
```python
import jax
import jax.numpy as jnp
from jax import lax
from jax.sharding import PartitionSpec as P

STOPS = 8
learn_rate = 0.005


def from_behind(block, axis, distance):
    devices = range(lax.axis_size(axis))
    route = [((i - distance) % len(devices), i) for i in devices]
    return lax.ppermute(block, axis, route)


def slot_index(rel_ids, nrel, most):
    ids = rel_ids[:, 0]
    onehot = (ids[:, None] == jnp.arange(nrel, dtype=jnp.int32)[None, :]).astype(jnp.int32)
    rank = jnp.cumsum(onehot, axis=0) - onehot
    return ids * most + jnp.sum(rank * onehot, axis=1)


def place_rows(rows, slot, total):
    return jnp.zeros((total, rows.shape[1]), rows.dtype).at[slot].set(rows)


def shards(source_rows, rel_ids, relations, entities, pos_slot, negatives):
    src_rows, width = source_rows.shape
    rel_dev = relations.shape[0]
    owners = lax.axis_size("rel")
    nrel = rel_dev * owners
    most = 2 * src_rows // nrel
    slot = slot_index(rel_ids, nrel, most)
    sent = place_rows(source_rows, slot, nrel * most).reshape(nrel, most, width)
    every_matrix = lax.all_gather(relations, "rel", axis=0, tiled=True)
    q_slots = jnp.einsum(
        "kmd,kde->kme", sent, every_matrix, preferred_element_type=jnp.float32
    ).astype(jnp.bfloat16)
    queries = q_slots.reshape(nrel * most, width)[slot]
    part_rows = entities.shape[0]
    columns = jnp.arange(part_rows, dtype=jnp.int32)
    state = entities
    query_acc = jnp.zeros((src_rows, width), jnp.float32)
    for stop in range(STOPS):
        if stop > 0:
            state = from_behind(state, "cand", 1)
        wide = state.astype(jnp.bfloat16)
        logits = lax.dot_general(
            queries, wide, (((1,), (1,)), ((), ())), preferred_element_type=jnp.float32
        )
        picks = negatives[stop]
        counts = jnp.zeros(logits.shape, jnp.float32)
        for sample in range(picks.shape[1]):
            counts = counts + (picks[:, sample][:, None] == columns[None, :]).astype(jnp.float32)
        hits = (pos_slot[:, None] == stop * part_rows + columns[None, :]).astype(jnp.float32)
        weight = (counts * jax.nn.sigmoid(logits) - hits * jax.nn.sigmoid(-logits)).astype(
            jnp.bfloat16
        )
        query_acc = query_acc + jnp.dot(weight, wide, preferred_element_type=jnp.float32)
        change = lax.dot_general(
            weight, queries, (((0,), (0,)), ((), ())), preferred_element_type=jnp.float32
        )
        state = state - learn_rate * change
    query_grad = query_acc.astype(jnp.bfloat16)
    gq_slots = place_rows(query_grad, slot, nrel * most).reshape(nrel, most, width)
    back_slots = jnp.einsum(
        "kme,kde->kmd", gq_slots, every_matrix, preferred_element_type=jnp.float32
    ).astype(jnp.bfloat16)
    terms = jnp.einsum("kmd,kme->dke", sent, gq_slots, preferred_element_type=jnp.float32)
    partial_value = lax.psum_scatter(
        terms.astype(jnp.bfloat16), "rel", scatter_dimension=1, tiled=True
    )
    source_grad = back_slots.reshape(nrel * most, width)[slot]
    relation_grad = lax.psum_scatter(partial_value, "cand", scatter_dimension=0, tiled=True).astype(
        jnp.float32
    )
    return (state, source_grad, relation_grad)


def solution(mesh):
    placed = (
        P(("cand", "rel"), None),
        P(("cand", "rel"), None),
        P("rel", None, None),
        P(("cand", "rel"), None),
        P(("cand", "rel")),
        P(None, ("cand", "rel"), None),
    )
    return jax.shard_map(
        shards,
        mesh=mesh,
        in_specs=placed,
        out_specs=(P(("cand", "rel"), None), P(("cand", "rel"), None), P("cand", "rel", None)),
        check_vma=False,
    )
```

profile of v0, /device:TPU:1, one launch (start us, length us, event | category | flops | bytes accessed | tf_op | source)
XLA Modules:
  0.0 535.6 jit_solution(7300290726071133954)
XLA Ops:
  7.2 0.7 all-gather.2.cloned.1.call-update
  7.9 0.7 fusion.63
  8.7 4.5 reduce-window.6
  13.2 0.4 slice_reduce_fusion
  13.9 0.8 fusion.14
  14.7 0.7 compare_select_fusion
  15.4 12.6 %scatter_custom_fusion = bf16[4096,512]{1,0:T(8,128)(2,1)} fusion(s32[2048]{0:T(1024)S(1)} %bitcast.221, bf16[2048,512]{1,0:T(8,128)(2,1)} %param.6, bf16[]{:T(256)} %constant.14.clone.1), kind=kCustom, calls=%fused_computation.131 | custom fusion | bytes 4194816 | tf_op jit(solution)/shard_map/scatter | solution.py:24
  28.1 0.6 iota_add_fusion.6
  28.6 0.6 iota_add_fusion.5
  29.4 0.7 fusion.70
  30.2 0.7 fusion.69
  30.9 0.7 fusion.68
  31.6 0.7 fusion.67
  32.4 88.9 %all-gather.2.cloned.1.call-done = bf16[16,512,512]{2,1,0:T(8,128)(2,1)} async-done(((bf16[2,512,512]{2,1,0:T(8,128)(2,1)}), bf16[16,512,512]{2,1,0:T(8,128)(2,1)}) %all-gather.2.cloned.1.call-update) | async-done | bytes 8388624 | tf_op jit(solution)/shard_map/all_gather | solution.py:35
  121.2 9.2 %convolution_convert_fusion.1 = bf16[16,256,512]{2,1,0:T(8,128)(2,1)} fusion(bf16[16,256,512]{2,1,0:T(8,128)(2,1)} %bitcast.213, bf16[16,512,512]{2,1,0:T(8,128)(2,1)} %all-gather.2.cloned.1.call-done), kind=kOutput, calls=%fused_computation.7 | convolution fusion | flops 2149580800 | bytes 16777216 | tf_op jit(solution)/shard_map/kmd,kde->kme/dot_general | solution.py:36
  130.4 10.4 %gather_fusion = bf16[2048,512]{1,0:T(8,128)(2,1)S(1)} fusion(bf16[4096,512]{1,0:T(8,128)(2,1)} %bitcast.211, s32[2048]{0:T(1024)S(1)} %broadcast_clamp_fusion), kind=kCustom, calls=%fused_computation | custom fusion | bytes 4202496 | tf_op jit(solution)/shard_map/gather | solution.py:39
  140.8 5.2 subtract_convert_fusion.7
  146.2 0.7 fusion.11
  147.0 3.1 collective-permute-start
  150.1 6.0 %collective-permute-done = f32[256,512]{1,0:T(8,128)S(1)} collective-permute-done((f32[256,512]{1,0:T(8,128)S(1)}, f32[256,512]{1,0:T(8,128)S(1)}, u32[]{:S(2)}, u32[]{:S(2)}) %collective-permute-start) | collective-permute-done | bytes 524320 | tf_op jit(solution)/shard_map/ppermute | solution.py:13
  156.3 5.2 subtract_convert_fusion.6
  161.7 0.7 fusion.10
  162.4 2.6 collective-permute-start.1
  165.1 6.0 %collective-permute-done.1 = f32[256,512]{1,0:T(8,128)S(1)} collective-permute-done((f32[256,512]{1,0:T(8,128)S(1)}, f32[256,512]{1,0:T(8,128)S(1)}, u32[]{:S(2)}, u32[]{:S(2)}) %collective-permute-start.1) | collective-permute-done | bytes 524320 | tf_op jit(solution)/shard_map/ppermute | solution.py:13
  171.2 5.2 subtract_convert_fusion.5
  176.6 0.7 fusion.9
  177.3 2.6 collective-permute-start.2
  180.0 6.0 %collective-permute-done.2 = f32[256,512]{1,0:T(8,128)S(1)} collective-permute-done((f32[256,512]{1,0:T(8,128)S(1)}, f32[256,512]{1,0:T(8,128)S(1)}, u32[]{:S(2)}, u32[]{:S(2)}) %collective-permute-start.2) | collective-permute-done | bytes 524320 | tf_op jit(solution)/shard_map/ppermute | solution.py:13
  186.2 5.2 subtract_convert_fusion.4
  191.3 0.7 fusion.8
  192.1 2.6 collective-permute-start.3
  194.8 2.8 fusion.57
  197.6 3.7 collective-permute-done.3
  201.4 5.2 subtract_convert_fusion.3
  206.6 0.7 fusion.7
  207.3 2.2 collective-permute-start.4
  209.6 2.7 fusion.51
  212.2 2.8 fusion.45
  215.0 3.3 collective-permute-done.4
  218.3 5.2 subtract_convert_fusion.2
  223.5 0.7 fusion.6
  224.3 2.7 fusion.39
  227.0 2.8 fusion.33
  229.8 5.2 collective-permute-done.5
  235.0 5.1 subtract_convert_fusion.1
  240.1 0.7 fusion.5
  240.9 0.3 collective-permute-start.6
  241.2 2.7 fusion.27
  243.8 2.8 fusion.21
  246.6 5.3 collective-permute-done.6
  251.9 5.2 subtract_convert_fusion
  257.1 2.7 fusion.15
  259.7 17.9 %scatter_custom_fusion.1 = bf16[4096,512]{1,0:T(8,128)(2,1)} fusion(s32[2048]{0:T(1024)} %bitcast.223, f32[2048,512]{1,0:T(8,128)} %fusion.15, f32[2048,512]{1,0:T(8,128)} %fusion.21, f32[2048,512]{1,0:T(8,128)} %fusion.27, f32[2048,512]{1,0:T(8,128)} %fusion.33, f32[2048,512]{1,0:T(8,128)} %fusion.39, f32[2048,512]{1,0:T(8,128)} %fusion.45, ...), kind=kCustom, calls=%fused_computation.8 | custom fusion | flops 8388608 | bytes 37749248 | tf_op jit(solution)/shard_map/scatter | solution.py:24
  277.6 9.1 %convert_bitcast_fusion = bf16[512,16,512]{0,2,1:T(8,128)(2,1)} fusion(bf16[16,256,512]{2,1,0:T(8,128)(2,1)} %bitcast.215, bf16[16,256,512]{2,1,0:T(8,128)(2,1)} %bitcast.214), kind=kOutput, calls=%fused_computation.4 | convolution fusion | flops 2151677952 | bytes 16777216 | tf_op jit(solution)/shard_map/kmd,kme->dke/dot_general | solution.py:69
  286.8 0.3 all-reduce.3.cloned.1.call-start
  287.1 0.3 copy-done.71
  287.4 0.6 dynamic-slice
  288.7 116.0 %reduce-scatter.2.cloned.1.call-done = bf16[512,2,512]{0,2,1:T(8,128)(2,1)} async-done(((bf16[512,16,512]{0,2,1:T(8,128)(2,1)}), bf16[512,2,512]{0,2,1:T(8,128)(2,1)}) %reduce-scatter.2.cloned.1.call-update) | async-done | bytes 1048592 | tf_op jit(solution)/shard_map/reduce_scatter | solution.py:70
  404.7 3.7 copy.14
  408.4 9.2 %convolution_convert_fusion = bf16[16,256,512]{2,1,0:T(8,128)(2,1)} fusion(bf16[16,256,512]{2,1,0:T(8,128)(2,1)} %bitcast.216, bf16[16,512,512]{2,1,0:T(8,128)(2,1)} %all-gather.2.cloned.1.call-done), kind=kOutput, calls=%fused_computation.6 | convolution fusion | flops 2149580800 | bytes 16777216 | tf_op jit(solution)/shard_map/kme,kde->kmd/dot_general | solution.py:66
  417.6 12.0 %gather_fusion.1 = bf16[2048,512]{1,0:T(8,128)(2,1)} fusion(bf16[4096,512]{1,0:T(8,128)(2,1)} %bitcast.212, s32[2048]{0:T(1024)S(1)} %copy-done.4), kind=kCustom, calls=%fused_computation.1 | custom fusion | bytes 4202496 | tf_op jit(solution)/shard_map/gather | solution.py:73
  429.6 2.6 fusion.4
  432.1 95.1 %all-reduce.3.cloned.1.call-done = bf16[512,2,512]{2,1,0:T(2,128)(2,1)} async-done(((bf16[512,2,512]{2,1,0:T(2,128)(2,1)}), bf16[512,2,512]{2,1,0:T(2,128)(2,1)}) %all-reduce.3.cloned.1.call-update) | async-done | bytes 1048592
  527.3 1.5 dynamic-slice_convert_fusion
  (165 shorter events, 1.2 us)
Async XLA Ops:
  7.2 114.1 %all-gather.2.cloned.1.call-start = ((), (), s32[]{:S(2)}) async-start(), calls=%async_computation.1 | async-start | bytes 9437184 | tf_op jit(solution)/shard_map/all_gather | solution.py:35
  7.9 396.8 %reduce-scatter.2.cloned.1.call-start = ((), (), s32[]{:S(2)}) async-start(), calls=%async_computation.2 | async-start | bytes 9437184 | tf_op jit(solution)/shard_map/reduce_scatter | solution.py:70
  15.4 13.8 %copy-start.5 = (s32[2048,1]{0,1:T(1,128)}, s32[2048,1]{0,1:T(1,128)S(1)}, u32[]{:S(2)}) copy-start(s32[2048,1]{0,1:T(1,128)S(1)} %compare_select_fusion) | copy-start | bytes 24580
  15.4 13.8 %copy-start = (s32[8,2048,16]{1,2,0:T(8,128)S(1)}, s32[8,2048,16]{1,2,0:T(8,128)}, u32[]{:S(2)}) copy-start(s32[8,2048,16]{1,2,0:T(8,128)} %param.11) | copy-start | bytes 3145732
  29.2 101.2 %copy-start.3 = (s32[2048]{0:T(1024)}, s32[2048]{0:T(1024)S(1)}, u32[]{:S(2)}) copy-start(s32[2048]{0:T(1024)S(1)} %broadcast_clamp_fusion) | copy-start | bytes 24580
  130.4 10.4 %copy-start.1 = (f32[256,512]{1,0:T(8,128)S(1)}, f32[256,512]{1,0:T(8,128)}, u32[]{:S(2)}) copy-start(f32[256,512]{1,0:T(8,128)} %param.9) | copy-start | bytes 1572868
  130.4 10.4 %copy-start.69 = (s32[2048]{0:T(1024)S(1)}, s32[2048]{0:T(1024)}, u32[]{:S(2)}) copy-start(s32[2048]{0:T(1024)} %param.10) | copy-start | bytes 24580
  146.0 10.1 %copy-start.53 = (s32[2048,1]{0,1:T(1,128)S(1)}, s32[2048,1]{0,1:T(1,128)}, u32[]{:S(2)}) copy-start(s32[2048,1]{0,1:T(1,128)} %get-tuple-element.113) | copy-start | bytes 24580
  146.0 10.1 %copy-start.54 = (s32[2048,1]{0,1:T(1,128)S(1)}, s32[2048,1]{0,1:T(1,128)}, u32[]{:S(2)}) copy-start(s32[2048,1]{0,1:T(1,128)} %get-tuple-element.114) | copy-start | bytes 24580
  146.1 10.1 %copy-start.55 = (s32[2048,1]{0,1:T(1,128)S(1)}, s32[2048,1]{0,1:T(1,128)}, u32[]{:S(2)}) copy-start(s32[2048,1]{0,1:T(1,128)} %get-tuple-element.115) | copy-start | bytes 24580
  146.1 10.1 %copy-start.56 = (s32[2048,1]{0,1:T(1,128)S(1)}, s32[2048,1]{0,1:T(1,128)}, u32[]{:S(2)}) copy-start(s32[2048,1]{0,1:T(1,128)} %get-tuple-element.116) | copy-start | bytes 24580
  146.1 10.1 %copy-start.57 = (s32[2048,1]{0,1:T(1,128)S(1)}, s32[2048,1]{0,1:T(1,128)}, u32[]{:S(2)}) copy-start(s32[2048,1]{0,1:T(1,128)} %get-tuple-element.117) | copy-start | bytes 24580
  146.1 10.1 %copy-start.58 = (s32[2048,1]{0,1:T(1,128)S(1)}, s32[2048,1]{0,1:T(1,128)}, u32[]{:S(2)}) copy-start(s32[2048,1]{0,1:T(1,128)} %get-tuple-element.118) | copy-start | bytes 24580
  146.1 10.1 %copy-start.59 = (s32[2048,1]{0,1:T(1,128)S(1)}, s32[2048,1]{0,1:T(1,128)}, u32[]{:S(2)}) copy-start(s32[2048,1]{0,1:T(1,128)} %get-tuple-element.119) | copy-start | bytes 24580
  146.1 10.1 %copy-start.60 = (s32[2048,1]{0,1:T(1,128)S(1)}, s32[2048,1]{0,1:T(1,128)}, u32[]{:S(2)}) copy-start(s32[2048,1]{0,1:T(1,128)} %get-tuple-element.120) | copy-start | bytes 24580
  146.1 10.1 %copy-start.61 = (s32[2048,1]{0,1:T(1,128)S(1)}, s32[2048,1]{0,1:T(1,128)}, u32[]{:S(2)}) copy-start(s32[2048,1]{0,1:T(1,128)} %get-tuple-element.121) | copy-start | bytes 24580
  146.1 10.1 %copy-start.62 = (s32[2048,1]{0,1:T(1,128)S(1)}, s32[2048,1]{0,1:T(1,128)}, u32[]{:S(2)}) copy-start(s32[2048,1]{0,1:T(1,128)} %get-tuple-element.122) | copy-start | bytes 24580
  146.1 10.1 %copy-start.63 = (s32[2048,1]{0,1:T(1,128)S(1)}, s32[2048,1]{0,1:T(1,128)}, u32[]{:S(2)}) copy-start(s32[2048,1]{0,1:T(1,128)} %get-tuple-element.123) | copy-start | bytes 24580
  146.1 10.1 %copy-start.64 = (s32[2048,1]{0,1:T(1,128)S(1)}, s32[2048,1]{0,1:T(1,128)}, u32[]{:S(2)}) copy-start(s32[2048,1]{0,1:T(1,128)} %get-tuple-element.124) | copy-start | bytes 24580
  146.2 10.1 %copy-start.65 = (s32[2048,1]{0,1:T(1,128)S(1)}, s32[2048,1]{0,1:T(1,128)}, u32[]{:S(2)}) copy-start(s32[2048,1]{0,1:T(1,128)} %get-tuple-element.125) | copy-start | bytes 24580
  146.2 10.1 %copy-start.66 = (s32[2048,1]{0,1:T(1,128)S(1)}, s32[2048,1]{0,1:T(1,128)}, u32[]{:S(2)}) copy-start(s32[2048,1]{0,1:T(1,128)} %get-tuple-element.126) | copy-start | bytes 24580
  146.2 10.1 %copy-start.67 = (s32[2048,1]{0,1:T(1,128)S(1)}, s32[2048,1]{0,1:T(1,128)}, u32[]{:S(2)}) copy-start(s32[2048,1]{0,1:T(1,128)} %get-tuple-element.127) | copy-start | bytes 24580
  146.2 10.1 %copy-start.68 = (s32[2048,1]{0,1:T(1,128)S(1)}, s32[2048,1]{0,1:T(1,128)}, u32[]{:S(2)}) copy-start(s32[2048,1]{0,1:T(1,128)} %get-tuple-element.128) | copy-start | bytes 24580
  146.2 10.1 %copy-start.70 = (s32[2048]{0:T(1024)S(1)}, s32[2048]{0:T(1024)}, u32[]{:S(2)}) copy-start(s32[2048]{0:T(1024)} %param.10) | copy-start | bytes 24580
  146.2 10.1 %copy-start.73 = (s32[256]{0:T(256)S(1)}, s32[256]{0:T(256)}, u32[]{:S(2)}) copy-start(s32[256]{0:T(256)} %iota_add_fusion.6) | copy-start | bytes 3076
  147.0 9.2 %collective-permute-start = (f32[256,512]{1,0:T(8,128)S(1)}, f32[256,512]{1,0:T(8,128)S(1)}, u32[]{:S(2)}, u32[]{:S(2)}) collective-permute-start(f32[256,512]{1,0:T(8,128)S(1)} %fusion.11), channel_id=1, source_target_pairs={{120,0},{0,8},{8,16},{16,24},{24,32},{32,40},{40,48},{48,56},{56,6... | collective-permute-start | bytes 1572872 | tf_op jit(solution)/shard_map/ppermute | solution.py:13
  161.5 9.6 %copy-start.37 = (s32[2048,1]{0,1:T(1,128)S(1)}, s32[2048,1]{0,1:T(1,128)}, u32[]{:S(2)}) copy-start(s32[2048,1]{0,1:T(1,128)} %get-tuple-element.97) | copy-start | bytes 24580
  161.5 9.6 %copy-start.38 = (s32[2048,1]{0,1:T(1,128)S(1)}, s32[2048,1]{0,1:T(1,128)}, u32[]{:S(2)}) copy-start(s32[2048,1]{0,1:T(1,128)} %get-tuple-element.98) | copy-start | bytes 24580
  161.5 9.6 %copy-start.39 = (s32[2048,1]{0,1:T(1,128)S(1)}, s32[2048,1]{0,1:T(1,128)}, u32[]{:S(2)}) copy-start(s32[2048,1]{0,1:T(1,128)} %get-tuple-element.99) | copy-start | bytes 24580
  161.5 9.6 %copy-start.40 = (s32[2048,1]{0,1:T(1,128)S(1)}, s32[2048,1]{0,1:T(1,128)}, u32[]{:S(2)}) copy-start(s32[2048,1]{0,1:T(1,128)} %get-tuple-element.100) | copy-start | bytes 24580
  161.6 9.6 %copy-start.41 = (s32[2048,1]{0,1:T(1,128)S(1)}, s32[2048,1]{0,1:T(1,128)}, u32[]{:S(2)}) copy-start(s32[2048,1]{0,1:T(1,128)} %get-tuple-element.101) | copy-start | bytes 24580
  161.6 9.6 %copy-start.42 = (s32[2048,1]{0,1:T(1,128)S(1)}, s32[2048,1]{0,1:T(1,128)}, u32[]{:S(2)}) copy-start(s32[2048,1]{0,1:T(1,128)} %get-tuple-element.102) | copy-start | bytes 24580
  161.6 9.6 %copy-start.43 = (s32[2048,1]{0,1:T(1,128)S(1)}, s32[2048,1]{0,1:T(1,128)}, u32[]{:S(2)}) copy-start(s32[2048,1]{0,1:T(1,128)} %get-tuple-element.103) | copy-start | bytes 24580
  161.6 9.6 %copy-start.44 = (s32[2048,1]{0,1:T(1,128)S(1)}, s32[2048,1]{0,1:T(1,128)}, u32[]{:S(2)}) copy-start(s32[2048,1]{0,1:T(1,128)} %get-tuple-element.104) | copy-start | bytes 24580
  161.6 9.6 %copy-start.45 = (s32[2048,1]{0,1:T(1,128)S(1)}, s32[2048,1]{0,1:T(1,128)}, u32[]{:S(2)}) copy-start(s32[2048,1]{0,1:T(1,128)} %get-tuple-element.105) | copy-start | bytes 24580
  161.6 9.6 %copy-start.46 = (s32[2048,1]{0,1:T(1,128)S(1)}, s32[2048,1]{0,1:T(1,128)}, u32[]{:S(2)}) copy-start(s32[2048,1]{0,1:T(1,128)} %get-tuple-element.106) | copy-start | bytes 24580
  161.6 9.6 %copy-start.47 = (s32[2048,1]{0,1:T(1,128)S(1)}, s32[2048,1]{0,1:T(1,128)}, u32[]{:S(2)}) copy-start(s32[2048,1]{0,1:T(1,128)} %get-tuple-element.107) | copy-start | bytes 24580
  161.6 9.6 %copy-start.48 = (s32[2048,1]{0,1:T(1,128)S(1)}, s32[2048,1]{0,1:T(1,128)}, u32[]{:S(2)}) copy-start(s32[2048,1]{0,1:T(1,128)} %get-tuple-element.108) | copy-start | bytes 24580
  161.6 9.6 %copy-start.49 = (s32[2048,1]{0,1:T(1,128)S(1)}, s32[2048,1]{0,1:T(1,128)}, u32[]{:S(2)}) copy-start(s32[2048,1]{0,1:T(1,128)} %get-tuple-element.109) | copy-start | bytes 24580
  161.6 9.6 %copy-start.50 = (s32[2048,1]{0,1:T(1,128)S(1)}, s32[2048,1]{0,1:T(1,128)}, u32[]{:S(2)}) copy-start(s32[2048,1]{0,1:T(1,128)} %get-tuple-element.110) | copy-start | bytes 24580
  161.7 9.6 %copy-start.51 = (s32[2048,1]{0,1:T(1,128)S(1)}, s32[2048,1]{0,1:T(1,128)}, u32[]{:S(2)}) copy-start(s32[2048,1]{0,1:T(1,128)} %get-tuple-element.111) | copy-start | bytes 24580
  161.7 9.6 %copy-start.52 = (s32[2048,1]{0,1:T(1,128)S(1)}, s32[2048,1]{0,1:T(1,128)}, u32[]{:S(2)}) copy-start(s32[2048,1]{0,1:T(1,128)} %get-tuple-element.112) | copy-start | bytes 24580
  161.7 9.6 %copy-start.72 = (s32[256]{0:T(256)S(1)}, s32[256]{0:T(256)}, u32[]{:S(2)}) copy-start(s32[256]{0:T(256)} %iota_add_fusion.5) | copy-start | bytes 3076
  162.4 8.7 %collective-permute-start.1 = (f32[256,512]{1,0:T(8,128)S(1)}, f32[256,512]{1,0:T(8,128)S(1)}, u32[]{:S(2)}, u32[]{:S(2)}) collective-permute-start(f32[256,512]{1,0:T(8,128)S(1)} %fusion.10), channel_id=1, source_target_pairs={{120,0},{0,8},{8,16},{16,24},{24,32},{32,40},{40,48},{48,56},{56,6... | collective-permute-start | bytes 1572872 | tf_op jit(solution)/shard_map/ppermute | solution.py:13
  176.4 9.6 %copy-start.21 = (s32[2048,1]{0,1:T(1,128)S(1)}, s32[2048,1]{0,1:T(1,128)}, u32[]{:S(2)}) copy-start(s32[2048,1]{0,1:T(1,128)} %get-tuple-element.81) | copy-start | bytes 24580
  176.5 9.6 %copy-start.22 = (s32[2048,1]{0,1:T(1,128)S(1)}, s32[2048,1]{0,1:T(1,128)}, u32[]{:S(2)}) copy-start(s32[2048,1]{0,1:T(1,128)} %get-tuple-element.82) | copy-start | bytes 24580
  176.5 9.6 %copy-start.23 = (s32[2048,1]{0,1:T(1,128)S(1)}, s32[2048,1]{0,1:T(1,128)}, u32[]{:S(2)}) copy-start(s32[2048,1]{0,1:T(1,128)} %get-tuple-element.83) | copy-start | bytes 24580
  176.5 9.6 %copy-start.24 = (s32[2048,1]{0,1:T(1,128)S(1)}, s32[2048,1]{0,1:T(1,128)}, u32[]{:S(2)}) copy-start(s32[2048,1]{0,1:T(1,128)} %get-tuple-element.84) | copy-start | bytes 24580
  176.5 9.6 %copy-start.25 = (s32[2048,1]{0,1:T(1,128)S(1)}, s32[2048,1]{0,1:T(1,128)}, u32[]{:S(2)}) copy-start(s32[2048,1]{0,1:T(1,128)} %get-tuple-element.85) | copy-start | bytes 24580
  176.5 9.6 %copy-start.26 = (s32[2048,1]{0,1:T(1,128)S(1)}, s32[2048,1]{0,1:T(1,128)}, u32[]{:S(2)}) copy-start(s32[2048,1]{0,1:T(1,128)} %get-tuple-element.86) | copy-start | bytes 24580
  176.5 9.6 %copy-start.27 = (s32[2048,1]{0,1:T(1,128)S(1)}, s32[2048,1]{0,1:T(1,128)}, u32[]{:S(2)}) copy-start(s32[2048,1]{0,1:T(1,128)} %get-tuple-element.87) | copy-start | bytes 24580
  176.5 9.6 %copy-start.28 = (s32[2048,1]{0,1:T(1,128)S(1)}, s32[2048,1]{0,1:T(1,128)}, u32[]{:S(2)}) copy-start(s32[2048,1]{0,1:T(1,128)} %get-tuple-element.88) | copy-start | bytes 24580
  176.5 9.6 %copy-start.29 = (s32[2048,1]{0,1:T(1,128)S(1)}, s32[2048,1]{0,1:T(1,128)}, u32[]{:S(2)}) copy-start(s32[2048,1]{0,1:T(1,128)} %get-tuple-element.89) | copy-start | bytes 24580
  176.5 9.6 %copy-start.30 = (s32[2048,1]{0,1:T(1,128)S(1)}, s32[2048,1]{0,1:T(1,128)}, u32[]{:S(2)}) copy-start(s32[2048,1]{0,1:T(1,128)} %get-tuple-element.90) | copy-start | bytes 24580
  176.5 9.6 %copy-start.31 = (s32[2048,1]{0,1:T(1,128)S(1)}, s32[2048,1]{0,1:T(1,128)}, u32[]{:S(2)}) copy-start(s32[2048,1]{0,1:T(1,128)} %get-tuple-element.91) | copy-start | bytes 24580
  176.6 9.6 %copy-start.32 = (s32[2048,1]{0,1:T(1,128)S(1)}, s32[2048,1]{0,1:T(1,128)}, u32[]{:S(2)}) copy-start(s32[2048,1]{0,1:T(1,128)} %get-tuple-element.92) | copy-start | bytes 24580
  176.6 9.6 %copy-start.33 = (s32[2048,1]{0,1:T(1,128)S(1)}, s32[2048,1]{0,1:T(1,128)}, u32[]{:S(2)}) copy-start(s32[2048,1]{0,1:T(1,128)} %get-tuple-element.93) | copy-start | bytes 24580
  176.6 9.6 %copy-start.34 = (s32[2048,1]{0,1:T(1,128)S(1)}, s32[2048,1]{0,1:T(1,128)}, u32[]{:S(2)}) copy-start(s32[2048,1]{0,1:T(1,128)} %get-tuple-element.94) | copy-start | bytes 24580
  177.3 8.7 %collective-permute-start.2 = (f32[256,512]{1,0:T(8,128)S(1)}, f32[256,512]{1,0:T(8,128)S(1)}, u32[]{:S(2)}, u32[]{:S(2)}) collective-permute-start(f32[256,512]{1,0:T(8,128)S(1)} %fusion.9), channel_id=1, source_target_pairs={{120,0},{0,8},{8,16},{16,24},{24,32},{32,40},{40,48},{48,56},{56,6... | collective-permute-start | bytes 1572872 | tf_op jit(solution)/shard_map/ppermute | solution.py:13
  192.1 9.2 %collective-permute-start.3 = (f32[256,512]{1,0:T(8,128)S(1)}, f32[256,512]{1,0:T(8,128)S(1)}, u32[]{:S(2)}, u32[]{:S(2)}) collective-permute-start(f32[256,512]{1,0:T(8,128)S(1)} %fusion.8), channel_id=1, source_target_pairs={{120,0},{0,8},{8,16},{16,24},{24,32},{32,40},{40,48},{48,56},{56,6... | collective-permute-start | bytes 1572872 | tf_op jit(solution)/shard_map/ppermute | solution.py:13
  207.3 11.0 %collective-permute-start.4 = (f32[256,512]{1,0:T(8,128)S(1)}, f32[256,512]{1,0:T(8,128)S(1)}, u32[]{:S(2)}, u32[]{:S(2)}) collective-permute-start(f32[256,512]{1,0:T(8,128)S(1)} %fusion.7), channel_id=1, source_target_pairs={{120,0},{0,8},{8,16},{16,24},{24,32},{32,40},{40,48},{48,56},{56,6... | collective-permute-start | bytes 1572872 | tf_op jit(solution)/shard_map/ppermute | solution.py:13
  224.2 10.8 %collective-permute-start.5 = (f32[256,512]{1,0:T(8,128)S(1)}, f32[256,512]{1,0:T(8,128)S(1)}, u32[]{:S(2)}, u32[]{:S(2)}) collective-permute-start(f32[256,512]{1,0:T(8,128)S(1)} %fusion.6), channel_id=1, source_target_pairs={{120,0},{0,8},{8,16},{16,24},{24,32},{32,40},{40,48},{48,56},{56,6... | collective-permute-start | bytes 1572872 | tf_op jit(solution)/shard_map/ppermute | solution.py:13
  240.9 11.0 %collective-permute-start.6 = (f32[256,512]{1,0:T(8,128)S(1)}, f32[256,512]{1,0:T(8,128)S(1)}, u32[]{:S(2)}, u32[]{:S(2)}) collective-permute-start(f32[256,512]{1,0:T(8,128)S(1)} %fusion.5), channel_id=1, source_target_pairs={{120,0},{0,8},{8,16},{16,24},{24,32},{32,40},{40,48},{48,56},{56,6... | collective-permute-start | bytes 1572872 | tf_op jit(solution)/shard_map/ppermute | solution.py:13
  286.8 240.4 %all-reduce.3.cloned.1.call-start = ((), (), s32[]{:S(2)}) async-start(), calls=%async_computation.3 | async-start | bytes 2097152
  (20 other events, 133.6 us)
Sparse Core Ops, SparseCore 0:
  10.3 110.8 all-gather.1
  286.9 117.7 reduce-scatter.1
  408.5 118.7 all-reduce.2
where the time goes:
time: 544 us; the launch traced here: 536 us
  waiting for transfers between devices  336 us (62%)
  matrix products  98.4 us (18%)
  local copies, waits for them, and re-layouts  43.7 us (8%)
  other arithmetic  27.7 us (5%)
  between operations  15.9 us (3%)
  starting transfers between devices  13.7 us (3%)
    reduce_scatter x1, waiting for transfers between devices, shards(): lax.psum_scatter(terms.astype(jnp.bfloat16), 'rel', scatter_dimension=1,...  116 us
    unnamed x4, waiting for transfers between devices  95.8 us
    all_gather x1, waiting for transfers between devices, shards(): every_matrix = lax.all_gather(relations, 'rel', axis=0, tiled=True)  88.9 us
    dot_general x8, matrix products, shards(): lax.dot_general(queries, wide, (((1,), (1,)), ((), ())), preferred_elemen...  41.4 us
    ppermute x7, waiting for transfers between devices, from_behind(): return lax.ppermute(block, axis, route)  35.6 us
    dot_general x8, matrix products, shards(): jnp.dot(weight, wide, preferred_element_type=jnp.float32)  21.8 us
    scatter x1, other arithmetic, place_rows(): return jnp.zeros((total, rows.shape[1]), rows.dtype).at[slot].set(rows)  17.9 us
    ppermute x7, starting transfers between devices, from_behind(): return lax.ppermute(block, axis, route)  13.3 us
  transfers between devices with their start and end apart: 10, of which 10 were waited for; matrix products, arithmetic and copies ran while one was open for 13% of the time, Pallas kernels for 0%

commit v1 on v0

--- a/solution.py
+++ b/solution.py
@@ -32,7 +32,9 @@
     most = 2 * src_rows // nrel
     slot = slot_index(rel_ids, nrel, most)
     sent = place_rows(source_rows, slot, nrel * most).reshape(nrel, most, width)
-    every_matrix = lax.all_gather(relations, "rel", axis=0, tiled=True)
+    every_matrix = jnp.concatenate(
+        lax.all_to_all(jnp.stack([relations] * lax.axis_size("rel")), "rel", 0, 0), axis=0
+    )
     q_slots = jnp.einsum(
         "kmd,kde->kme", sent, every_matrix, preferred_element_type=jnp.float32
     ).astype(jnp.bfloat16)

time: 544 us -> 571 us (1.050)
  waiting for transfers between devices: 336 us -> 352 us
  starting transfers between devices: 13.7 us -> 21.3 us
    all_gather x1 -> x0, waiting for transfers between devices: 88.9 us -> none  [shards(): every_matrix = lax.all_gather(relations, 'rel', axis=0, tiled=True)]
    all_to_all x0 -> x1, waiting for transfers between devices: none -> 73.7 us  [shards(): lax.all_to_all(jnp.stack([relations] * lax.axis_size('rel')), 'rel', 0, 0)]
    reduce_scatter x1, waiting for transfers between devices: 116 us -> 148 us  [shards(): lax.psum_scatter(terms.astype(jnp.bfloat16), 'rel', scatter_dimension=1,...]
    all_to_all x0 -> x1, starting transfers between devices: none -> 8.28 us  [shards(): lax.all_to_all(jnp.stack([relations] * lax.axis_size('rel')), 'rel', 0, 0)]
    unnamed x4 -> x3, waiting for transfers between devices: 95.8 us -> 95 us
  transfers between devices with their start and end apart: 10 -> 10, of which waited for: 10 -> 10; matrix products, arithmetic and copies ran while one was open for 13% -> 12% of each run, Pallas kernels for 0% -> 0%
where the time goes in v1:
time: 571 us; the launch traced here: 563 us
  waiting for transfers between devices  352 us (62%)
  matrix products  98.4 us (17%)
  local copies, waits for them, and re-layouts  49 us (9%)
  other arithmetic  25.5 us (4%)
  starting transfers between devices  21.3 us (4%)
  between operations  16.4 us (3%)
    reduce_scatter x1, waiting for transfers between devices, shards(): lax.psum_scatter(terms.astype(jnp.bfloat16), 'rel', scatter_dimension=1,...  148 us
    unnamed x3, waiting for transfers between devices  95 us
    all_to_all x1, waiting for transfers between devices, shards(): lax.all_to_all(jnp.stack([relations] * lax.axis_size('rel')), 'rel', 0, 0)  73.7 us
    dot_general x8, matrix products, shards(): lax.dot_general(queries, wide, (((1,), (1,)), ((), ())), preferred_elemen...  41.4 us
    ppermute x7, waiting for transfers between devices, from_behind(): return lax.ppermute(block, axis, route)  35.4 us
    dot_general x8, matrix products, shards(): jnp.dot(weight, wide, preferred_element_type=jnp.float32)  21.8 us
    scatter x1, other arithmetic, place_rows(): return jnp.zeros((total, rows.shape[1]), rows.dtype).at[slot].set(rows)  17.9 us
    ppermute x7, starting transfers between devices, from_behind(): return lax.ppermute(block, axis, route)  12.6 us
  transfers between devices with their start and end apart: 10, of which 10 were waited for; matrix products, arithmetic and copies ran while one was open for 12% of the time, Pallas kernels for 0%

profile of v1, /device:TPU:1, one launch (start us, length us, event | category | flops | bytes accessed | tf_op | source)
XLA Modules:
  0.0 562.6 jit_solution(3673270064968379309)
XLA Ops:
  7.2 5.3 stack.2
  12.5 8.3 %all-to-all-start = ((bf16[8,2,512,512]{3,2,1,0:T(8,128)(2,1)}), bf16[8,2,512,512]{3,2,1,0:T(8,128)(2,1)}, u32[]{:S(2)}, u32[]{:S(2)}) async-start(bf16[8,2,512,512]{3,2,1,0:T(8,128)(2,1)} %stack.2), calls=%async_computation | async-start | bytes 16777216 | tf_op jit(solution)/shard_map/all_to_all | solution.py:36
  20.9 4.5 reduce-window.6
  25.4 0.4 slice_reduce_fusion
  25.8 0.2 reduce-window.9
  26.0 0.1 broadcast_add_fusion
  26.2 12.6 %scatter_custom_fusion = bf16[4096,512]{1,0:T(8,128)(2,1)} fusion(s32[2048]{0:T(1024)S(1)} %bitcast.222, bf16[2048,512]{1,0:T(8,128)(2,1)} %param.6, bf16[]{:T(256)} %constant.14.clone.1), kind=kCustom, calls=%fused_computation.131 | custom fusion | bytes 4194816 | tf_op jit(solution)/shard_map/scatter | solution.py:24
  38.9 0.5 iota_add_fusion.6
  39.4 0.6 iota_add_fusion.5
  40.2 0.7 fusion.70
  40.9 0.8 fusion.69
  41.7 0.7 fusion.68
  42.4 0.7 fusion.67
  43.2 73.7 %all-to-all-done = bf16[8,2,512,512]{3,2,1,0:T(8,128)(2,1)} async-done(((bf16[8,2,512,512]{3,2,1,0:T(8,128)(2,1)}), bf16[8,2,512,512]{3,2,1,0:T(8,128)(2,1)}, u32[]{:S(2)}, u32[]{:S(2)}) %all-to-all-start) | async-done | bytes 8388640 | tf_op jit(solution)/shard_map/all_to_all | solution.py:36
  116.9 9.2 %convolution_convert_fusion.1 = bf16[16,256,512]{2,1,0:T(8,128)(2,1)} fusion(bf16[16,256,512]{2,1,0:T(8,128)(2,1)} %bitcast.214, bf16[16,512,512]{2,1,0:T(8,128)(2,1)} %bitcast.23), kind=kOutput, calls=%fused_computation.7 | convolution fusion | flops 2149580800 | bytes 16777216 | tf_op jit(solution)/shard_map/kmd,kde->kme/dot_general | solution.py:38
  126.1 10.4 %gather_fusion = bf16[2048,512]{1,0:T(8,128)(2,1)S(1)} fusion(bf16[4096,512]{1,0:T(8,128)(2,1)} %bitcast.212, s32[2048]{0:T(1024)S(1)} %broadcast_clamp_fusion), kind=kCustom, calls=%fused_computation | custom fusion | bytes 4202496 | tf_op jit(solution)/shard_map/gather | solution.py:41
  136.5 5.2 subtract_convert_fusion.7
  141.9 0.7 fusion.11
  142.6 2.2 collective-permute-start
  144.9 6.0 %collective-permute-done = f32[256,512]{1,0:T(8,128)S(1)} collective-permute-done((f32[256,512]{1,0:T(8,128)S(1)}, f32[256,512]{1,0:T(8,128)S(1)}, u32[]{:S(2)}, u32[]{:S(2)}) %collective-permute-start) | collective-permute-done | bytes 524320 | tf_op jit(solution)/shard_map/ppermute | solution.py:13
  151.1 5.2 subtract_convert_fusion.6
  156.5 0.7 fusion.10
  157.2 2.6 collective-permute-start.1
  159.9 6.0 %collective-permute-done.1 = f32[256,512]{1,0:T(8,128)S(1)} collective-permute-done((f32[256,512]{1,0:T(8,128)S(1)}, f32[256,512]{1,0:T(8,128)S(1)}, u32[]{:S(2)}, u32[]{:S(2)}) %collective-permute-start.1) | collective-permute-done | bytes 524320 | tf_op jit(solution)/shard_map/ppermute | solution.py:13
  166.0 5.2 subtract_convert_fusion.5
  171.4 0.7 fusion.9
  172.1 2.6 collective-permute-start.2
  174.8 6.0 %collective-permute-done.2 = f32[256,512]{1,0:T(8,128)S(1)} collective-permute-done((f32[256,512]{1,0:T(8,128)S(1)}, f32[256,512]{1,0:T(8,128)S(1)}, u32[]{:S(2)}, u32[]{:S(2)}) %collective-permute-start.2) | collective-permute-done | bytes 524320 | tf_op jit(solution)/shard_map/ppermute | solution.py:13
  180.9 5.2 subtract_convert_fusion.4
  186.1 0.7 fusion.8
  186.9 2.6 collective-permute-start.3
  189.6 2.8 fusion.57
  192.4 3.6 collective-permute-done.3
  196.1 5.2 subtract_convert_fusion.3
  201.3 0.7 fusion.7
  202.0 2.3 collective-permute-start.4
  204.4 2.7 fusion.51
  207.0 2.8 fusion.45
  209.8 3.2 collective-permute-done.4
  213.0 5.2 subtract_convert_fusion.2
  218.2 0.7 fusion.6
  219.0 2.7 fusion.39
  221.7 2.8 fusion.33
  224.5 5.2 collective-permute-done.5
  229.7 5.1 subtract_convert_fusion.1
  234.9 0.7 fusion.5
  235.6 0.3 collective-permute-start.6
  236.0 2.6 fusion.27
  238.6 2.8 fusion.21
  241.4 5.3 collective-permute-done.6
  246.7 5.2 subtract_convert_fusion
  251.8 2.7 fusion.15
  254.5 17.9 %scatter_custom_fusion.1 = bf16[4096,512]{1,0:T(8,128)(2,1)} fusion(s32[2048]{0:T(1024)} %bitcast.224, f32[2048,512]{1,0:T(8,128)} %fusion.15, f32[2048,512]{1,0:T(8,128)} %fusion.21, f32[2048,512]{1,0:T(8,128)} %fusion.27, f32[2048,512]{1,0:T(8,128)} %fusion.33, f32[2048,512]{1,0:T(8,128)} %fusion.39, f32[2048,512]{1,0:T(8,128)} %fusion.45, ...), kind=kCustom, calls=%fused_computation.8 | custom fusion | flops 8388608 | bytes 37749248 | tf_op jit(solution)/shard_map/scatter | solution.py:24
  272.4 9.1 %convert_bitcast_fusion = bf16[512,16,512]{0,2,1:T(8,128)(2,1)} fusion(bf16[16,256,512]{2,1,0:T(8,128)(2,1)} %bitcast.216, bf16[16,256,512]{2,1,0:T(8,128)(2,1)} %bitcast.215), kind=kOutput, calls=%fused_computation.4 | convolution fusion | flops 2151677952 | bytes 16777216 | tf_op jit(solution)/shard_map/kmd,kme->dke/dot_general | solution.py:71
  281.6 0.3 all-reduce.3.cloned.1.call-start
  281.9 0.3 copy-done.72
  282.2 0.6 dynamic-slice
  283.5 147.9 %reduce-scatter.2.cloned.1.call-done = bf16[512,2,512]{0,2,1:T(8,128)(2,1)} async-done(((bf16[512,16,512]{0,2,1:T(8,128)(2,1)}), bf16[512,2,512]{0,2,1:T(8,128)(2,1)}) %reduce-scatter.2.cloned.1.call-update) | async-done | bytes 1048592 | tf_op jit(solution)/shard_map/reduce_scatter | solution.py:72
  431.4 3.7 copy.14
  435.1 9.2 %convolution_convert_fusion = bf16[16,256,512]{2,1,0:T(8,128)(2,1)} fusion(bf16[16,256,512]{2,1,0:T(8,128)(2,1)} %bitcast.217, bf16[16,512,512]{2,1,0:T(8,128)(2,1)} %bitcast.23), kind=kOutput, calls=%fused_computation.6 | convolution fusion | flops 2149580800 | bytes 16777216 | tf_op jit(solution)/shard_map/kme,kde->kmd/dot_general | solution.py:68
  444.3 12.0 %gather_fusion.1 = bf16[2048,512]{1,0:T(8,128)(2,1)} fusion(bf16[4096,512]{1,0:T(8,128)(2,1)} %bitcast.213, s32[2048]{0:T(1024)S(1)} %copy-done.4), kind=kCustom, calls=%fused_computation.1 | custom fusion | bytes 4202496 | tf_op jit(solution)/shard_map/gather | solution.py:75
  456.3 2.6 fusion.4
  458.8 94.9 %all-reduce.3.cloned.1.call-done = bf16[512,2,512]{2,1,0:T(2,128)(2,1)} async-done(((bf16[512,2,512]{2,1,0:T(2,128)(2,1)}), bf16[512,2,512]{2,1,0:T(2,128)(2,1)}) %all-reduce.3.cloned.1.call-update) | async-done | bytes 1048592
  553.7 1.5 dynamic-slice_convert_fusion
  (167 shorter events, 1.0 us)
Async XLA Ops:
  12.5 104.4 %all-to-all-start = ((bf16[8,2,512,512]{3,2,1,0:T(8,128)(2,1)}), bf16[8,2,512,512]{3,2,1,0:T(8,128)(2,1)}, u32[]{:S(2)}, u32[]{:S(2)}) async-start(bf16[8,2,512,512]{3,2,1,0:T(8,128)(2,1)} %stack.2), calls=%async_computation | async-start | bytes 16777216 | tf_op jit(solution)/shard_map/all_to_all | solution.py:36
  20.8 410.6 %reduce-scatter.2.cloned.1.call-start = ((), (), s32[]{:S(2)}) async-start(), calls=%async_computation.2 | async-start | bytes 9437184 | tf_op jit(solution)/shard_map/reduce_scatter | solution.py:72
  26.2 13.7 %copy-start.6 = (s32[2048,1]{0,1:T(1,128)}, s32[2048,1]{0,1:T(1,128)S(1)}, u32[]{:S(2)}) copy-start(s32[2048,1]{0,1:T(1,128)S(1)} %compare_select_fusion) | copy-start | bytes 24580
  26.2 13.7 %copy-start = (s32[8,2048,16]{1,2,0:T(8,128)S(1)}, s32[8,2048,16]{1,2,0:T(8,128)}, u32[]{:S(2)}) copy-start(s32[8,2048,16]{1,2,0:T(8,128)} %param.11) | copy-start | bytes 3145732
  40.0 86.1 %copy-start.3 = (s32[2048]{0:T(1024)}, s32[2048]{0:T(1024)S(1)}, u32[]{:S(2)}) copy-start(s32[2048]{0:T(1024)S(1)} %broadcast_clamp_fusion) | copy-start | bytes 24580
  126.1 10.4 %copy-start.1 = (f32[256,512]{1,0:T(8,128)S(1)}, f32[256,512]{1,0:T(8,128)}, u32[]{:S(2)}) copy-start(f32[256,512]{1,0:T(8,128)} %param.9) | copy-start | bytes 1572868
  126.1 10.4 %copy-start.70 = (s32[2048]{0:T(1024)S(1)}, s32[2048]{0:T(1024)}, u32[]{:S(2)}) copy-start(s32[2048]{0:T(1024)} %param.10) | copy-start | bytes 24580
  141.7 9.3 %copy-start.54 = (s32[2048,1]{0,1:T(1,128)S(1)}, s32[2048,1]{0,1:T(1,128)}, u32[]{:S(2)}) copy-start(s32[2048,1]{0,1:T(1,128)} %get-tuple-element.113) | copy-start | bytes 24580
  141.7 9.3 %copy-start.55 = (s32[2048,1]{0,1:T(1,128)S(1)}, s32[2048,1]{0,1:T(1,128)}, u32[]{:S(2)}) copy-start(s32[2048,1]{0,1:T(1,128)} %get-tuple-element.114) | copy-start | bytes 24580
  141.7 9.2 %copy-start.56 = (s32[2048,1]{0,1:T(1,128)S(1)}, s32[2048,1]{0,1:T(1,128)}, u32[]{:S(2)}) copy-start(s32[2048,1]{0,1:T(1,128)} %get-tuple-element.115) | copy-start | bytes 24580
  141.7 9.2 %copy-start.57 = (s32[2048,1]{0,1:T(1,128)S(1)}, s32[2048,1]{0,1:T(1,128)}, u32[]{:S(2)}) copy-start(s32[2048,1]{0,1:T(1,128)} %get-tuple-element.116) | copy-start | bytes 24580
  141.7 9.2 %copy-start.58 = (s32[2048,1]{0,1:T(1,128)S(1)}, s32[2048,1]{0,1:T(1,128)}, u32[]{:S(2)}) copy-start(s32[2048,1]{0,1:T(1,128)} %get-tuple-element.117) | copy-start | bytes 24580
  141.7 9.2 %copy-start.59 = (s32[2048,1]{0,1:T(1,128)S(1)}, s32[2048,1]{0,1:T(1,128)}, u32[]{:S(2)}) copy-start(s32[2048,1]{0,1:T(1,128)} %get-tuple-element.118) | copy-start | bytes 24580
  141.8 9.2 %copy-start.60 = (s32[2048,1]{0,1:T(1,128)S(1)}, s32[2048,1]{0,1:T(1,128)}, u32[]{:S(2)}) copy-start(s32[2048,1]{0,1:T(1,128)} %get-tuple-element.119) | copy-start | bytes 24580
  141.8 9.2 %copy-start.61 = (s32[2048,1]{0,1:T(1,128)S(1)}, s32[2048,1]{0,1:T(1,128)}, u32[]{:S(2)}) copy-start(s32[2048,1]{0,1:T(1,128)} %get-tuple-element.120) | copy-start | bytes 24580
  141.8 9.2 %copy-start.62 = (s32[2048,1]{0,1:T(1,128)S(1)}, s32[2048,1]{0,1:T(1,128)}, u32[]{:S(2)}) copy-start(s32[2048,1]{0,1:T(1,128)} %get-tuple-element.121) | copy-start | bytes 24580
  141.8 9.2 %copy-start.63 = (s32[2048,1]{0,1:T(1,128)S(1)}, s32[2048,1]{0,1:T(1,128)}, u32[]{:S(2)}) copy-start(s32[2048,1]{0,1:T(1,128)} %get-tuple-element.122) | copy-start | bytes 24580
  141.8 9.2 %copy-start.64 = (s32[2048,1]{0,1:T(1,128)S(1)}, s32[2048,1]{0,1:T(1,128)}, u32[]{:S(2)}) copy-start(s32[2048,1]{0,1:T(1,128)} %get-tuple-element.123) | copy-start | bytes 24580
  141.8 9.2 %copy-start.65 = (s32[2048,1]{0,1:T(1,128)S(1)}, s32[2048,1]{0,1:T(1,128)}, u32[]{:S(2)}) copy-start(s32[2048,1]{0,1:T(1,128)} %get-tuple-element.124) | copy-start | bytes 24580
  141.8 9.2 %copy-start.66 = (s32[2048,1]{0,1:T(1,128)S(1)}, s32[2048,1]{0,1:T(1,128)}, u32[]{:S(2)}) copy-start(s32[2048,1]{0,1:T(1,128)} %get-tuple-element.125) | copy-start | bytes 24580
  141.8 9.2 %copy-start.67 = (s32[2048,1]{0,1:T(1,128)S(1)}, s32[2048,1]{0,1:T(1,128)}, u32[]{:S(2)}) copy-start(s32[2048,1]{0,1:T(1,128)} %get-tuple-element.126) | copy-start | bytes 24580
  141.8 9.2 %copy-start.68 = (s32[2048,1]{0,1:T(1,128)S(1)}, s32[2048,1]{0,1:T(1,128)}, u32[]{:S(2)}) copy-start(s32[2048,1]{0,1:T(1,128)} %get-tuple-element.127) | copy-start | bytes 24580
  141.8 9.2 %copy-start.69 = (s32[2048,1]{0,1:T(1,128)S(1)}, s32[2048,1]{0,1:T(1,128)}, u32[]{:S(2)}) copy-start(s32[2048,1]{0,1:T(1,128)} %get-tuple-element.128) | copy-start | bytes 24580
  142.6 8.3 %collective-permute-start = (f32[256,512]{1,0:T(8,128)S(1)}, f32[256,512]{1,0:T(8,128)S(1)}, u32[]{:S(2)}, u32[]{:S(2)}) collective-permute-start(f32[256,512]{1,0:T(8,128)S(1)} %fusion.11), channel_id=1, source_target_pairs={{120,0},{0,8},{8,16},{16,24},{24,32},{32,40},{40,48},{48,56},{56,6... | collective-permute-start | bytes 1572872 | tf_op jit(solution)/shard_map/ppermute | solution.py:13
  156.3 9.6 %copy-start.38 = (s32[2048,1]{0,1:T(1,128)S(1)}, s32[2048,1]{0,1:T(1,128)}, u32[]{:S(2)}) copy-start(s32[2048,1]{0,1:T(1,128)} %get-tuple-element.97) | copy-start | bytes 24580
  156.3 9.6 %copy-start.39 = (s32[2048,1]{0,1:T(1,128)S(1)}, s32[2048,1]{0,1:T(1,128)}, u32[]{:S(2)}) copy-start(s32[2048,1]{0,1:T(1,128)} %get-tuple-element.98) | copy-start | bytes 24580
  156.3 9.6 %copy-start.40 = (s32[2048,1]{0,1:T(1,128)S(1)}, s32[2048,1]{0,1:T(1,128)}, u32[]{:S(2)}) copy-start(s32[2048,1]{0,1:T(1,128)} %get-tuple-element.99) | copy-start | bytes 24580
  156.3 9.6 %copy-start.41 = (s32[2048,1]{0,1:T(1,128)S(1)}, s32[2048,1]{0,1:T(1,128)}, u32[]{:S(2)}) copy-start(s32[2048,1]{0,1:T(1,128)} %get-tuple-element.100) | copy-start | bytes 24580
  156.3 9.6 %copy-start.42 = (s32[2048,1]{0,1:T(1,128)S(1)}, s32[2048,1]{0,1:T(1,128)}, u32[]{:S(2)}) copy-start(s32[2048,1]{0,1:T(1,128)} %get-tuple-element.101) | copy-start | bytes 24580
  156.4 9.6 %copy-start.43 = (s32[2048,1]{0,1:T(1,128)S(1)}, s32[2048,1]{0,1:T(1,128)}, u32[]{:S(2)}) copy-start(s32[2048,1]{0,1:T(1,128)} %get-tuple-element.102) | copy-start | bytes 24580
  156.4 9.6 %copy-start.44 = (s32[2048,1]{0,1:T(1,128)S(1)}, s32[2048,1]{0,1:T(1,128)}, u32[]{:S(2)}) copy-start(s32[2048,1]{0,1:T(1,128)} %get-tuple-element.103) | copy-start | bytes 24580
  156.4 9.6 %copy-start.45 = (s32[2048,1]{0,1:T(1,128)S(1)}, s32[2048,1]{0,1:T(1,128)}, u32[]{:S(2)}) copy-start(s32[2048,1]{0,1:T(1,128)} %get-tuple-element.104) | copy-start | bytes 24580
  156.4 9.6 %copy-start.46 = (s32[2048,1]{0,1:T(1,128)S(1)}, s32[2048,1]{0,1:T(1,128)}, u32[]{:S(2)}) copy-start(s32[2048,1]{0,1:T(1,128)} %get-tuple-element.105) | copy-start | bytes 24580
  156.4 9.6 %copy-start.47 = (s32[2048,1]{0,1:T(1,128)S(1)}, s32[2048,1]{0,1:T(1,128)}, u32[]{:S(2)}) copy-start(s32[2048,1]{0,1:T(1,128)} %get-tuple-element.106) | copy-start | bytes 24580
  156.4 9.6 %copy-start.48 = (s32[2048,1]{0,1:T(1,128)S(1)}, s32[2048,1]{0,1:T(1,128)}, u32[]{:S(2)}) copy-start(s32[2048,1]{0,1:T(1,128)} %get-tuple-element.107) | copy-start | bytes 24580
  156.4 9.6 %copy-start.49 = (s32[2048,1]{0,1:T(1,128)S(1)}, s32[2048,1]{0,1:T(1,128)}, u32[]{:S(2)}) copy-start(s32[2048,1]{0,1:T(1,128)} %get-tuple-element.108) | copy-start | bytes 24580
  156.4 9.6 %copy-start.50 = (s32[2048,1]{0,1:T(1,128)S(1)}, s32[2048,1]{0,1:T(1,128)}, u32[]{:S(2)}) copy-start(s32[2048,1]{0,1:T(1,128)} %get-tuple-element.109) | copy-start | bytes 24580
  156.4 9.6 %copy-start.51 = (s32[2048,1]{0,1:T(1,128)S(1)}, s32[2048,1]{0,1:T(1,128)}, u32[]{:S(2)}) copy-start(s32[2048,1]{0,1:T(1,128)} %get-tuple-element.110) | copy-start | bytes 24580
  156.4 9.6 %copy-start.52 = (s32[2048,1]{0,1:T(1,128)S(1)}, s32[2048,1]{0,1:T(1,128)}, u32[]{:S(2)}) copy-start(s32[2048,1]{0,1:T(1,128)} %get-tuple-element.111) | copy-start | bytes 24580
  156.5 9.6 %copy-start.53 = (s32[2048,1]{0,1:T(1,128)S(1)}, s32[2048,1]{0,1:T(1,128)}, u32[]{:S(2)}) copy-start(s32[2048,1]{0,1:T(1,128)} %get-tuple-element.112) | copy-start | bytes 24580
  156.5 9.6 %copy-start.73 = (s32[256]{0:T(256)S(1)}, s32[256]{0:T(256)}, u32[]{:S(2)}) copy-start(s32[256]{0:T(256)} %iota_add_fusion.5) | copy-start | bytes 3076
  157.2 8.7 %collective-permute-start.1 = (f32[256,512]{1,0:T(8,128)S(1)}, f32[256,512]{1,0:T(8,128)S(1)}, u32[]{:S(2)}, u32[]{:S(2)}) collective-permute-start(f32[256,512]{1,0:T(8,128)S(1)} %fusion.10), channel_id=1, source_target_pairs={{120,0},{0,8},{8,16},{16,24},{24,32},{32,40},{40,48},{48,56},{56,6... | collective-permute-start | bytes 1572872 | tf_op jit(solution)/shard_map/ppermute | solution.py:13
  171.2 9.6 %copy-start.22 = (s32[2048,1]{0,1:T(1,128)S(1)}, s32[2048,1]{0,1:T(1,128)}, u32[]{:S(2)}) copy-start(s32[2048,1]{0,1:T(1,128)} %get-tuple-element.81) | copy-start | bytes 24580
  171.2 9.6 %copy-start.23 = (s32[2048,1]{0,1:T(1,128)S(1)}, s32[2048,1]{0,1:T(1,128)}, u32[]{:S(2)}) copy-start(s32[2048,1]{0,1:T(1,128)} %get-tuple-element.82) | copy-start | bytes 24580
  171.3 9.6 %copy-start.24 = (s32[2048,1]{0,1:T(1,128)S(1)}, s32[2048,1]{0,1:T(1,128)}, u32[]{:S(2)}) copy-start(s32[2048,1]{0,1:T(1,128)} %get-tuple-element.83) | copy-start | bytes 24580
  171.3 9.6 %copy-start.25 = (s32[2048,1]{0,1:T(1,128)S(1)}, s32[2048,1]{0,1:T(1,128)}, u32[]{:S(2)}) copy-start(s32[2048,1]{0,1:T(1,128)} %get-tuple-element.84) | copy-start | bytes 24580
  171.3 9.6 %copy-start.26 = (s32[2048,1]{0,1:T(1,128)S(1)}, s32[2048,1]{0,1:T(1,128)}, u32[]{:S(2)}) copy-start(s32[2048,1]{0,1:T(1,128)} %get-tuple-element.85) | copy-start | bytes 24580
  171.3 9.6 %copy-start.27 = (s32[2048,1]{0,1:T(1,128)S(1)}, s32[2048,1]{0,1:T(1,128)}, u32[]{:S(2)}) copy-start(s32[2048,1]{0,1:T(1,128)} %get-tuple-element.86) | copy-start | bytes 24580
  171.3 9.6 %copy-start.28 = (s32[2048,1]{0,1:T(1,128)S(1)}, s32[2048,1]{0,1:T(1,128)}, u32[]{:S(2)}) copy-start(s32[2048,1]{0,1:T(1,128)} %get-tuple-element.87) | copy-start | bytes 24580
  171.3 9.6 %copy-start.29 = (s32[2048,1]{0,1:T(1,128)S(1)}, s32[2048,1]{0,1:T(1,128)}, u32[]{:S(2)}) copy-start(s32[2048,1]{0,1:T(1,128)} %get-tuple-element.88) | copy-start | bytes 24580
  171.3 9.6 %copy-start.30 = (s32[2048,1]{0,1:T(1,128)S(1)}, s32[2048,1]{0,1:T(1,128)}, u32[]{:S(2)}) copy-start(s32[2048,1]{0,1:T(1,128)} %get-tuple-element.89) | copy-start | bytes 24580
  171.3 9.6 %copy-start.31 = (s32[2048,1]{0,1:T(1,128)S(1)}, s32[2048,1]{0,1:T(1,128)}, u32[]{:S(2)}) copy-start(s32[2048,1]{0,1:T(1,128)} %get-tuple-element.90) | copy-start | bytes 24580
  171.3 9.6 %copy-start.32 = (s32[2048,1]{0,1:T(1,128)S(1)}, s32[2048,1]{0,1:T(1,128)}, u32[]{:S(2)}) copy-start(s32[2048,1]{0,1:T(1,128)} %get-tuple-element.91) | copy-start | bytes 24580
  171.3 9.6 %copy-start.33 = (s32[2048,1]{0,1:T(1,128)S(1)}, s32[2048,1]{0,1:T(1,128)}, u32[]{:S(2)}) copy-start(s32[2048,1]{0,1:T(1,128)} %get-tuple-element.92) | copy-start | bytes 24580
  171.4 9.6 %copy-start.34 = (s32[2048,1]{0,1:T(1,128)S(1)}, s32[2048,1]{0,1:T(1,128)}, u32[]{:S(2)}) copy-start(s32[2048,1]{0,1:T(1,128)} %get-tuple-element.93) | copy-start | bytes 24580
  171.4 9.6 %copy-start.35 = (s32[2048,1]{0,1:T(1,128)S(1)}, s32[2048,1]{0,1:T(1,128)}, u32[]{:S(2)}) copy-start(s32[2048,1]{0,1:T(1,128)} %get-tuple-element.94) | copy-start | bytes 24580
  171.4 9.6 %copy-start.36 = (s32[2048,1]{0,1:T(1,128)S(1)}, s32[2048,1]{0,1:T(1,128)}, u32[]{:S(2)}) copy-start(s32[2048,1]{0,1:T(1,128)} %get-tuple-element.95) | copy-start | bytes 24580
  171.4 9.6 %copy-start.37 = (s32[2048,1]{0,1:T(1,128)S(1)}, s32[2048,1]{0,1:T(1,128)}, u32[]{:S(2)}) copy-start(s32[2048,1]{0,1:T(1,128)} %get-tuple-element.96) | copy-start | bytes 24580
  172.1 8.7 %collective-permute-start.2 = (f32[256,512]{1,0:T(8,128)S(1)}, f32[256,512]{1,0:T(8,128)S(1)}, u32[]{:S(2)}, u32[]{:S(2)}) collective-permute-start(f32[256,512]{1,0:T(8,128)S(1)} %fusion.9), channel_id=1, source_target_pairs={{120,0},{0,8},{8,16},{16,24},{24,32},{32,40},{40,48},{48,56},{56,6... | collective-permute-start | bytes 1572872 | tf_op jit(solution)/shard_map/ppermute | solution.py:13
  186.9 9.1 %collective-permute-start.3 = (f32[256,512]{1,0:T(8,128)S(1)}, f32[256,512]{1,0:T(8,128)S(1)}, u32[]{:S(2)}, u32[]{:S(2)}) collective-permute-start(f32[256,512]{1,0:T(8,128)S(1)} %fusion.8), channel_id=1, source_target_pairs={{120,0},{0,8},{8,16},{16,24},{24,32},{32,40},{40,48},{48,56},{56,6... | collective-permute-start | bytes 1572872 | tf_op jit(solution)/shard_map/ppermute | solution.py:13
  202.0 11.0 %collective-permute-start.4 = (f32[256,512]{1,0:T(8,128)S(1)}, f32[256,512]{1,0:T(8,128)S(1)}, u32[]{:S(2)}, u32[]{:S(2)}) collective-permute-start(f32[256,512]{1,0:T(8,128)S(1)} %fusion.7), channel_id=1, source_target_pairs={{120,0},{0,8},{8,16},{16,24},{24,32},{32,40},{40,48},{48,56},{56,6... | collective-permute-start | bytes 1572872 | tf_op jit(solution)/shard_map/ppermute | solution.py:13
  218.9 10.8 %collective-permute-start.5 = (f32[256,512]{1,0:T(8,128)S(1)}, f32[256,512]{1,0:T(8,128)S(1)}, u32[]{:S(2)}, u32[]{:S(2)}) collective-permute-start(f32[256,512]{1,0:T(8,128)S(1)} %fusion.6), channel_id=1, source_target_pairs={{120,0},{0,8},{8,16},{16,24},{24,32},{32,40},{40,48},{48,56},{56,6... | collective-permute-start | bytes 1572872 | tf_op jit(solution)/shard_map/ppermute | solution.py:13
  235.6 11.0 %collective-permute-start.6 = (f32[256,512]{1,0:T(8,128)S(1)}, f32[256,512]{1,0:T(8,128)S(1)}, u32[]{:S(2)}, u32[]{:S(2)}) collective-permute-start(f32[256,512]{1,0:T(8,128)S(1)} %fusion.5), channel_id=1, source_target_pairs={{120,0},{0,8},{8,16},{16,24},{24,32},{32,40},{40,48},{48,56},{56,6... | collective-permute-start | bytes 1572872 | tf_op jit(solution)/shard_map/ppermute | solution.py:13
  281.6 272.1 %all-reduce.3.cloned.1.call-start = ((), (), s32[]{:S(2)}) async-start(), calls=%async_computation.3 | async-start | bytes 2097152
  (21 other events, 139.9 us)
Sparse Core Ops, SparseCore 0:
  281.7 149.6 reduce-scatter.1
  435.2 118.5 all-reduce.2
